TPU v7x, 32 devices: a whole 2x2x4 slice. The times are simulated.
32 devices in a mesh: side: 2 (over core), group: 8 (over z, y), head: 2 (over x).
Axes of the slice: x: 2, y: 2, z: 4, core: 2. Of those that a mesh axis runs over, the one named last changes fastest.
Arguments:
- pool_rows: bfloat16 [2, 768, 4096], P('side', ('group', 'head')), may hold values from -24 to 24
- pool_weight: bfloat16 [2, 4096, 8192], P('side', 'group', 'head'), as said below
- lengths: int32 [8, 3], replicated, may hold values from 1 to 48, 96 in all within a row
- owner: int32 [8, 3], replicated, may hold values from 0 to 7, as said below
Outputs:
- pool_out: bfloat16 [2, 768, 4096], P('side', 'group', 'head')
Inputs may be any that keep to these rules, and one draw needn't show every extreme that they name: owner[p, j] is p with the binary digits of m_j flipped, where m_j = owner[0, j] is the same for every p; the m_j differ between slots, and every binary digit below 8 is set in some m_j. So the 3 requests of a prefill group go to different decode groups, and every decode group receives exactly one request for each slot j. `lengths`: each row sums to 96. `pool_weight`: independent normal entries of deviation 1 / sqrt(4096).
All inputs are finite; a program needn't handle non-finite values.
Results may differ from a plain program's by a relative error of at most 0.0061.
Values may be sent and summed in bfloat16 or wider, within the bound.
A program may use at most 128 MiB of HBM per device.

v0:
```python
import jax
import jax.numpy as jnp
from jax import lax
from jax.sharding import PartitionSpec as P

HEAD_DIM = 256


def shifted(value, axis, by):
    count = lax.axis_size(axis)
    pairs = [(i, i + by) for i in range(count) if 0 <= i + by < count]
    return lax.ppermute(value, axis, pairs)


def on_device(pool_rows, pool_weight, lengths, owner):
    side_index = lax.axis_index("side")
    group_index = lax.axis_index("group")
    requests = lengths.shape[1]
    gathered = lax.all_gather(pool_rows[0], "head", axis=0, tiled=True)
    weight = lax.all_gather(pool_weight[0], "group", axis=0, tiled=True)
    mem_g = gathered.shape[0]
    wide = weight.shape[1] // 2
    heads_dev = wide // HEAD_DIM
    q_req = mem_g // requests
    scale = 1.0 / HEAD_DIM**0.5
    cached = jnp.dot(gathered, weight, preferred_element_type=jnp.float32).astype(jnp.bfloat16)
    queries = cached[:, :wide]
    starts = jnp.cumsum(lengths, axis=1) - lengths
    groups = jnp.arange(lengths.shape[0], dtype=jnp.int32)
    sources, begins, counts = ([], [], [])
    for slot in range(requests):
        hit = owner[:, slot] == group_index
        sources.append(jnp.sum(jnp.where(hit, groups, 0)))
        begins.append(jnp.sum(jnp.where(hit, starts[:, slot], 0)))
        counts.append(jnp.sum(jnp.where(hit, lengths[:, slot], 0)))
    moved = shifted(cached, "side", 1)
    row_slot = jnp.arange(mem_g, dtype=jnp.int32) // q_req
    lower = jnp.zeros((mem_g,), jnp.int32)
    upper = jnp.zeros((mem_g,), jnp.int32)
    for slot in range(requests):
        here = row_slot == slot
        first_row = sources[slot] * mem_g + begins[slot]
        lower = jnp.where(here, first_row, lower)
        upper = jnp.where(here, first_row + counts[slot], upper)
    query_heads = queries.reshape(mem_g, heads_dev, HEAD_DIM)
    piece = lax.all_gather(moved, "group", axis=0, tiled=True)
    running = jnp.full((heads_dev, mem_g), -1e30, jnp.float32)
    count_rows = piece.shape[0]
    key_index = jnp.arange(count_rows, dtype=jnp.int32)
    key_rows = piece[:, :wide].reshape(count_rows, heads_dev, HEAD_DIM)
    value_rows = piece[:, wide:].reshape(count_rows, heads_dev, HEAD_DIM)
    allowed = (key_index[None, :] >= lower[:, None]) & (key_index[None, :] < upper[:, None])
    scores = (
        jnp.einsum("qeh,keh->eqk", query_heads, key_rows, preferred_element_type=jnp.float32)
        * scale
    )
    scores = jnp.where(allowed[None], scores, -1e30)
    newest = jnp.maximum(running, jnp.max(scores, axis=-1))
    expo = jnp.where(allowed[None], jnp.exp(scores - newest[:, :, None]), 0.0)
    total = jnp.sum(expo, axis=-1)
    update = jnp.einsum(
        "eqk,keh->eqh", expo.astype(jnp.bfloat16), value_rows, preferred_element_type=jnp.float32
    )
    accum = update
    running, total, accum = (newest, total, accum)
    mixed = accum / total[:, :, None]
    attended = jnp.transpose(mixed, (1, 0, 2)).reshape(mem_g, wide).astype(jnp.bfloat16)
    partial_out = lax.dot_general(
        attended, weight[:, wide:], (((1,), (1,)), ((), ())), preferred_element_type=jnp.float32
    )
    decoded = lax.psum_scatter(partial_out, "head", scatter_dimension=1, tiled=True).astype(
        jnp.bfloat16
    )
    result = jnp.where(side_index == 0, cached[:, :wide], decoded)
    return result[None]


def solution(mesh):
    placed = (P("side", ("group", "head"), None), P("side", "group", "head"), P(), P())
    return jax.shard_map(
        on_device, mesh=mesh, in_specs=placed, out_specs=P("side", "group", "head"), check_vma=False
    )
```

profile of v0, /device:TPU:0, one launch (start us, length us, event | category | flops | bytes accessed | tf_op | source)
XLA Modules:
  0.0 815.8 jit_solution(10971161938531449910)
XLA Ops:
  6.5 0.0 copy-start.1
  6.5 0.0 all-gather.7.cloned.1.call-start
  6.5 0.7 all-gather.7.cloned.1.call-update
  7.3 0.0 all-gather.5.cloned.1.call-start
  7.3 0.2 copy-done.1
  7.5 12.7 %all-gather = bf16[1,96,4096]{2,1,0:T(8,128)(2,1)S(1)} all-gather(bf16[1,48,4096]{2,1,0:T(8,128)(2,1)S(1)} %copy-done.1), channel_id=2, replica_groups=mesh['side'=2,'group'=8,'head'=2] {'head'}, dimensions={1}, use_global_device_ids=true | all-gather | bytes 1179648 | tf_op jit(solution)/shard_map/all_gather | solution.py:19
  20.3 0.0 copy-start.2
  20.3 0.0 copy-start.3
  20.3 629.0 %all-gather.7.cloned.1.call-done = bf16[1,4096,4096]{2,1,0:T(8,128)(2,1)} async-done(((bf16[1,512,4096]{2,1,0:T(8,128)(2,1)}), bf16[1,4096,4096]{2,1,0:T(8,128)(2,1)}) %all-gather.7.cloned.1.call-update) | async-done | bytes 33554448 | tf_op jit(solution)/shard_map/all_gather | solution.py:20
  649.3 13.4 %convolution_convert_fusion = bf16[96,4096]{1,0:T(8,128)(2,1)S(1)} fusion(bf16[1,96,4096]{2,1,0:T(8,128)(2,1)S(1)} %all-gather, bf16[1,4096,4096]{2,1,0:T(8,128)(2,1)} %all-gather.7.cloned.1.call-done), kind=kOutput, calls=%fused_computation.2 | convolution fusion | flops 3221618688 | bytes 35127296 | tf_op jit(solution)/shard_map/dot_general | solution.py:26
  662.7 1.6 collective-permute-start
  664.3 1.8 collective-permute-done
  666.2 0.0 copy-start
  666.2 0.9 copy-done
  667.1 0.0 all-gather.5.cloned.1.call-update
  667.1 0.0 reduce-scatter.2.cloned.1.call-start
  667.2 0.0 copy-done.2
  667.2 0.0 copy-done.3
  667.2 0.8 fusion.41
  673.7 0.1 fusion.38
  673.9 92.4 %all-gather.5.cloned.1.call-done = bf16[768,4096]{1,0:T(8,128)(2,1)} async-done(((bf16[96,4096]{1,0:T(8,128)(2,1)}), bf16[768,4096]{1,0:T(8,128)(2,1)}) %all-gather.5.cloned.1.call-update) | async-done | bytes 6291472 | tf_op jit(solution)/shard_map/all_gather | solution.py:46
  766.3 3.4 fusion.52
  769.8 1.2 fusion.8
  771.0 0.8 fusion.9
  771.7 1.1 fusion.30
  772.9 9.9 %fusion = f32[96,4096]{1,0:T(8,128)} fusion(bf16[96,2048]{1,0:T(8,128)(2,1)S(1)} %bitcast.91, bf16[4096,4096]{1,0:T(8,128)(2,1)} %bitcast.87), kind=kOutput, calls=%fused_computation | convolution fusion | flops 1610612736 | bytes 18743296 | tf_op jit(solution)/shard_map/dot_general | solution.py:68
  782.8 0.0 reduce-scatter.2.cloned.1.call-update
  782.8 24.5 %reduce-scatter.2.cloned.1.call-done = f32[96,2048]{1,0:T(8,128)} async-done(((f32[96,4096]{1,0:T(8,128)}), f32[96,2048]{1,0:T(8,128)}) %reduce-scatter.2.cloned.1.call-update) | async-done | bytes 786448 | tf_op jit(solution)/shard_map/reduce_scatter | solution.py:71
  807.3 1.9 select_bitcast_fusion
  (6 shorter events, 0.1 us)
Async XLA Ops:
  6.5 1.0 copy-start.1
  6.5 642.8 %all-gather.7.cloned.1.call-start = ((), (), s32[]{:S(2)}) async-start(), calls=%async_computation.3 | async-start | bytes 37748736 | tf_op jit(solution)/shard_map/all_gather | solution.py:20
  7.3 759.1 %all-gather.5.cloned.1.call-start = ((), (), s32[]{:S(2)}) async-start(), calls=%async_computation.1 | async-start | bytes 7077888 | tf_op jit(solution)/shard_map/all_gather | solution.py:46
  20.3 646.9 %copy-start.2 = (s32[8,3]{0,1:T(4,128)S(1)}, s32[8,3]{0,1:T(4,128)}, u32[]{:S(2)}) copy-start(s32[8,3]{0,1:T(4,128)} %param.6) | copy-start | bytes 292
  20.3 647.0 %copy-start.3 = (s32[8,3]{0,1:T(4,128)S(1)}, s32[8,3]{0,1:T(4,128)}, u32[]{:S(2)}) copy-start(s32[8,3]{0,1:T(4,128)} %param.7) | copy-start | bytes 292
  662.7 3.5 collective-permute-start
  666.2 0.9 copy-start
  667.1 140.2 %reduce-scatter.2.cloned.1.call-start = ((), (), s32[]{:S(2)}) async-start(), calls=%async_computation.2 | async-start | bytes 2359296 | tf_op jit(solution)/shard_map/reduce_scatter | solution.py:71
Sparse Core Ops, SparseCore 0:
  8.9 640.3 all-gather.6
  667.3 99.0 all-gather.4
  782.9 24.3 reduce-scatter.1
where the time goes:
time: 816 us
  waiting for transfers between devices  749 us (92%)
  matrix products  25.6 us (3%)
  between operations  18.8 us (2%)
  blocking collectives  12.7 us (2%)
    all_gather x1, waiting for transfers between devices, on_device(): weight = lax.all_gather(pool_weight[0], 'group', axis=0, tiled=True)  629 us
    all_gather x1, waiting for transfers between devices, on_device(): piece = lax.all_gather(moved, 'group', axis=0, tiled=True)  92.4 us
    reduce_scatter x1, waiting for transfers between devices, on_device(): lax.psum_scatter(partial_out, 'head', scatter_dimension=1, tiled=True)  24.5 us
  transfers between devices with their start and end apart: 4, of which 4 were waited for; matrix products, arithmetic and copies ran while one was open for 0% of the time, Pallas kernels for 0%

commit v1 on v0

--- a/solution.py
+++ b/solution.py
@@ -17,7 +17,14 @@
     group_index = lax.axis_index("group")
     requests = lengths.shape[1]
     gathered = lax.all_gather(pool_rows[0], "head", axis=0, tiled=True)
-    weight = lax.all_gather(pool_weight[0], "group", axis=0, tiled=True)
+    ring = [pool_weight[0]]
+    for hop in range(7):
+        ring.append(lax.ppermute(ring[-1], "group", [(dev, (dev + 1) % 8) for dev in range(8)]))
+    weight = jnp.roll(
+        jnp.concatenate(ring[::-1], axis=0),
+        (lax.axis_index("group") + 1) * ring[0].shape[0],
+        axis=0,
+    )
     mem_g = gathered.shape[0]
     wide = weight.shape[1] // 2
     heads_dev = wide // HEAD_DIM

time: 816 us -> 886 us (1.086)
  local copies, waits for them, and re-layouts: 4.64 us -> 67 us
    ppermute x0 -> x7, waiting for transfers between devices: none -> 639 us  [on_device(): lax.ppermute(ring[-1], 'group', [(dev, (dev + 1) % 8) for dev in range(8)])]
    all_gather x1 -> x0, waiting for transfers between devices: 629 us -> none  [on_device(): weight = lax.all_gather(pool_weight[0], 'group', axis=0, tiled=True)]
    unnamed x8 -> x43, local copies, waits for them, and re-layouts: 1.16 us -> 61.3 us
  transfers between devices with their start and end apart: 4 -> 10, of which waited for: 4 -> 10; matrix products, arithmetic and copies ran while one was open for 0% -> 0% of each run, Pallas kernels for 0% -> 0%
where the time goes in v1:
time: 886 us; the launch traced here: 885 us
  waiting for transfers between devices  754 us (85%)
  local copies, waits for them, and re-layouts  67 us (8%)
  matrix products  28 us (3%)
  between operations  19.3 us (2%)
    ppermute x7, waiting for transfers between devices, on_device(): lax.ppermute(ring[-1], 'group', [(dev, (dev + 1) % 8) for dev in range(8)])  639 us
    all_gather x1, waiting for transfers between devices, on_device(): piece = lax.all_gather(moved, 'group', axis=0, tiled=True)  88.1 us
    unnamed x43, local copies, waits for them, and re-layouts  61.3 us
    reduce_scatter x1, waiting for transfers between devices, on_device(): lax.psum_scatter(partial_out, 'head', scatter_dimension=1, tiled=True)  24.5 us
  transfers between devices with their start and end apart: 10, of which 10 were waited for; matrix products, arithmetic and copies ran while one was open for 0% of the time, Pallas kernels for 0%

profile of v1, /device:TPU:0, one launch (start us, length us, event | category | flops | bytes accessed | tf_op | source)
XLA Modules:
  0.0 885.0 jit_solution(11832674673785233724)
XLA Ops:
  6.5 3.0 collective-permute-start
  9.5 93.8 %collective-permute-done = bf16[512,4096]{1,0:T(8,128)(2,1)S(1)} collective-permute-done((bf16[512,4096]{1,0:T(8,128)(2,1)}, bf16[512,4096]{1,0:T(8,128)(2,1)S(1)}, u32[]{:S(2)}, u32[]{:S(2)}) %collective-permute-start) | collective-permute-done | bytes 4194336 | tf_op jit(solution)/shard_map/ppermute | solution.py:22
  105.3 94.4 %collective-permute-done.1 = bf16[512,4096]{1,0:T(8,128)(2,1)S(1)} collective-permute-done((bf16[512,4096]{1,0:T(8,128)(2,1)S(1)}, bf16[512,4096]{1,0:T(8,128)(2,1)S(1)}, u32[]{:S(2)}, u32[]{:S(2)}) %collective-permute-start.1) | collective-permute-done | bytes 4194336 | tf_op jit(solution)/shard_map/ppermute | solution.py:22
  199.7 2.0 copy-done.3
  201.7 93.6 %collective-permute-done.2 = bf16[512,4096]{1,0:T(8,128)(2,1)S(1)} collective-permute-done((bf16[512,4096]{1,0:T(8,128)(2,1)S(1)}, bf16[512,4096]{1,0:T(8,128)(2,1)S(1)}, u32[]{:S(2)}, u32[]{:S(2)}) %collective-permute-start.2) | collective-permute-done | bytes 4194336 | tf_op jit(solution)/shard_map/ppermute | solution.py:22
  295.3 2.0 copy-done.5
  297.3 92.7 %collective-permute-done.3 = bf16[512,4096]{1,0:T(8,128)(2,1)S(1)} collective-permute-done((bf16[512,4096]{1,0:T(8,128)(2,1)S(1)}, bf16[512,4096]{1,0:T(8,128)(2,1)S(1)}, u32[]{:S(2)}, u32[]{:S(2)}) %collective-permute-start.3) | collective-permute-done | bytes 4194336 | tf_op jit(solution)/shard_map/ppermute | solution.py:22
  391.9 91.9 %collective-permute-done.4 = bf16[512,4096]{1,0:T(8,128)(2,1)S(1)} collective-permute-done((bf16[512,4096]{1,0:T(8,128)(2,1)S(1)}, bf16[512,4096]{1,0:T(8,128)(2,1)S(1)}, u32[]{:S(2)}, u32[]{:S(2)}) %collective-permute-start.4) | collective-permute-done | bytes 4194336 | tf_op jit(solution)/shard_map/ppermute | solution.py:22
  485.7 91.1 %collective-permute-done.5 = bf16[512,4096]{1,0:T(8,128)(2,1)} collective-permute-done((bf16[512,4096]{1,0:T(8,128)(2,1)S(1)}, bf16[512,4096]{1,0:T(8,128)(2,1)}, u32[]{:S(2)}, u32[]{:S(2)}) %collective-permute-start.5) | collective-permute-done | bytes 4194336 | tf_op jit(solution)/shard_map/ppermute | solution.py:22
  576.8 8.6 all-gather
  585.5 81.8 %collective-permute-done.6 = bf16[512,4096]{1,0:T(8,128)(2,1)} collective-permute-done((bf16[512,4096]{1,0:T(8,128)(2,1)}, bf16[512,4096]{1,0:T(8,128)(2,1)}, u32[]{:S(2)}, u32[]{:S(2)}) %collective-permute-start.6) | collective-permute-done | bytes 4194336 | tf_op jit(solution)/shard_map/ppermute | solution.py:22
  667.3 4.6 constant_dynamic-update-slice_fusion.15
  671.9 4.8 constant_dynamic-update-slice_fusion.14
  676.7 2.4 constant_dynamic-update-slice_fusion.13
  680.4 2.4 constant_dynamic-update-slice_fusion.12
  684.1 2.4 constant_dynamic-update-slice_fusion.11
  687.8 2.4 constant_dynamic-update-slice_fusion.10
  691.5 2.4 constant_dynamic-update-slice_fusion.9
  695.2 2.2 constant_dynamic-update-slice_fusion.8
  697.5 4.7 constant_dynamic-update-slice_fusion.7
  702.2 4.6 constant_dynamic-update-slice_fusion.6
  706.8 2.2 constant_dynamic-update-slice_fusion.5
  709.0 2.2 constant_dynamic-update-slice_fusion.4
  711.2 2.3 constant_dynamic-update-slice_fusion.3
  713.5 2.2 constant_dynamic-update-slice_fusion.2
  715.8 2.2 constant_dynamic-update-slice_fusion.1
  717.9 2.2 constant_dynamic-update-slice_fusion
  720.2 13.5 %fusion.7 = bf16[96,4096]{1,0:T(8,128)(2,1)S(1)} fusion(bf16[8192,4096]{1,0:T(8,128)(2,1)} %constant_dynamic-update-slice_fusion, s32[]{:T(128)S(6)} %select_n.123, bf16[1,96,4096]{2,1,0:T(8,128)(2,1)S(1)} %all-gather), kind=kOutput, calls=%fused_computation.5 | convolution fusion | flops 3221618688 | bytes 35127300 | tf_op jit(solution)/shard_map/dot_general | solution.py:33
  744.9 88.1 %all-gather.3.cloned.1.call-done = bf16[768,4096]{1,0:T(8,128)(2,1)} async-done(((bf16[96,4096]{1,0:T(8,128)(2,1)}), bf16[768,4096]{1,0:T(8,128)(2,1)}) %all-gather.3.cloned.1.call-update) | async-done | bytes 6291472 | tf_op jit(solution)/shard_map/all_gather | solution.py:53
  833.0 3.4 fusion.60
  839.5 12.2 %fusion.2 = f32[96,4096]{1,0:T(8,128)} fusion(bf16[96,2048]{1,0:T(8,128)(2,1)S(1)} %bitcast.93, bf16[8192,4096]{1,0:T(8,128)(2,1)} %constant_dynamic-update-slice_fusion, s32[]{:T(128)S(6)} %select_n.123, s32[]{:T(128)S(6)} %add.50), kind=kOutput, calls=%fused_computation.2 | convolution fusion | flops 1610612736 | bytes 18743304 | tf_op jit(solution)/shard_map/dot_general | solution.py:75
  851.7 24.5 %reduce-scatter.2.cloned.1.call-done = f32[96,2048]{1,0:T(8,128)} async-done(((f32[96,4096]{1,0:T(8,128)}), f32[96,2048]{1,0:T(8,128)}) %reduce-scatter.2.cloned.1.call-update) | async-done | bytes 786448 | tf_op jit(solution)/shard_map/reduce_scatter | solution.py:78
  (50 shorter events, 22.7 us)
Async XLA Ops:
  6.5 826.4 %all-gather.3.cloned.1.call-start = ((), (), s32[]{:S(2)}) async-start(), calls=%async_computation.1 | async-start | bytes 7077888 | tf_op jit(solution)/shard_map/all_gather | solution.py:53
  6.5 96.8 %collective-permute-start = (bf16[512,4096]{1,0:T(8,128)(2,1)}, bf16[512,4096]{1,0:T(8,128)(2,1)S(1)}, u32[]{:S(2)}, u32[]{:S(2)}) collective-permute-start(bf16[512,4096]{1,0:T(8,128)(2,1)} %bitcast.89), channel_id=1, source_target_pairs={{0,2},{2,4},{4,6},{6,8},{8,10},{10,12},{12,14},{14,0},{1,3},{3,5},... | collective-permute-start | bytes 12582920 | tf_op jit(solution)/shard_map/ppermute | solution.py:22
  103.3 2.0 copy-start.1
  105.3 94.4 %collective-permute-start.1 = (bf16[512,4096]{1,0:T(8,128)(2,1)S(1)}, bf16[512,4096]{1,0:T(8,128)(2,1)S(1)}, u32[]{:S(2)}, u32[]{:S(2)}) collective-permute-start(bf16[512,4096]{1,0:T(8,128)(2,1)S(1)} %collective-permute-done), channel_id=1, source_target_pairs={{0,2},{2,4},{4,6},{6,8},{8,10},{10,12},{12,14},{14,0},{1,3},{3,5},... | collective-permute-start | bytes 12582920 | tf_op jit(solution)/shard_map/ppermute | solution.py:22
  199.7 2.0 copy-start.3
  201.7 93.6 %collective-permute-start.2 = (bf16[512,4096]{1,0:T(8,128)(2,1)S(1)}, bf16[512,4096]{1,0:T(8,128)(2,1)S(1)}, u32[]{:S(2)}, u32[]{:S(2)}) collective-permute-start(bf16[512,4096]{1,0:T(8,128)(2,1)S(1)} %collective-permute-done.1), channel_id=1, source_target_pairs={{0,2},{2,4},{4,6},{6,8},{8,10},{10,12},{12,14},{14,0},{1,3},{3,5},... | collective-permute-start | bytes 12582920 | tf_op jit(solution)/shard_map/ppermute | solution.py:22
  295.3 2.0 copy-start.5
  297.3 92.7 %collective-permute-start.3 = (bf16[512,4096]{1,0:T(8,128)(2,1)S(1)}, bf16[512,4096]{1,0:T(8,128)(2,1)S(1)}, u32[]{:S(2)}, u32[]{:S(2)}) collective-permute-start(bf16[512,4096]{1,0:T(8,128)(2,1)S(1)} %collective-permute-done.2), channel_id=1, source_target_pairs={{0,2},{2,4},{4,6},{6,8},{8,10},{10,12},{12,14},{14,0},{1,3},{3,5},... | collective-permute-start | bytes 12582920 | tf_op jit(solution)/shard_map/ppermute | solution.py:22
  390.0 1.9 copy-start.7
  391.9 91.9 %collective-permute-start.4 = (bf16[512,4096]{1,0:T(8,128)(2,1)S(1)}, bf16[512,4096]{1,0:T(8,128)(2,1)S(1)}, u32[]{:S(2)}, u32[]{:S(2)}) collective-permute-start(bf16[512,4096]{1,0:T(8,128)(2,1)S(1)} %collective-permute-done.3), channel_id=1, source_target_pairs={{0,2},{2,4},{4,6},{6,8},{8,10},{10,12},{12,14},{14,0},{1,3},{3,5},... | collective-permute-start | bytes 12582920 | tf_op jit(solution)/shard_map/ppermute | solution.py:22
  483.8 1.9 copy-start.9
  485.7 91.1 %collective-permute-start.5 = (bf16[512,4096]{1,0:T(8,128)(2,1)S(1)}, bf16[512,4096]{1,0:T(8,128)(2,1)}, u32[]{:S(2)}, u32[]{:S(2)}) collective-permute-start(bf16[512,4096]{1,0:T(8,128)(2,1)S(1)} %collective-permute-done.4), channel_id=1, source_target_pairs={{0,2},{2,4},{4,6},{6,8},{8,10},{10,12},{12,14},{14,0},{1,3},{3,5},... | collective-permute-start | bytes 12582920 | tf_op jit(solution)/shard_map/ppermute | solution.py:22
  576.8 90.5 %collective-permute-start.6 = (bf16[512,4096]{1,0:T(8,128)(2,1)}, bf16[512,4096]{1,0:T(8,128)(2,1)}, u32[]{:S(2)}, u32[]{:S(2)}) collective-permute-start(bf16[512,4096]{1,0:T(8,128)(2,1)} %collective-permute-done.5), channel_id=1, source_target_pairs={{0,2},{2,4},{4,6},{6,8},{8,10},{10,12},{12,14},{14,0},{1,3},{3,5},... | collective-permute-start | bytes 12582920 | tf_op jit(solution)/shard_map/ppermute | solution.py:22
  671.9 4.8 copy-start.10
  676.7 3.7 copy-start.8
  680.4 3.7 copy-start.6
  684.1 3.7 copy-start.4
  687.8 3.7 copy-start.2
  691.5 3.7 copy-start
  720.1 17.9 %copy-start.12 = (s32[8,3]{0,1:T(4,128)S(1)}, s32[8,3]{0,1:T(4,128)}, u32[]{:S(2)}) copy-start(s32[8,3]{0,1:T(4,128)} %param.6) | copy-start | bytes 292
  720.2 18.0 %copy-start.13 = (s32[8,3]{0,1:T(4,128)S(1)}, s32[8,3]{0,1:T(4,128)}, u32[]{:S(2)}) copy-start(s32[8,3]{0,1:T(4,128)} %param.7) | copy-start | bytes 292
  733.7 3.2 collective-permute-start.7
  736.9 0.9 copy-start.11
  737.8 138.4 %reduce-scatter.2.cloned.1.call-start = ((), (), s32[]{:S(2)}) async-start(), calls=%async_computation.2 | async-start | bytes 2359296 | tf_op jit(solution)/shard_map/reduce_scatter | solution.py:78
Sparse Core Ops, SparseCore 0:
  737.9 94.9 all-gather.2
  851.9 24.3 reduce-scatter.1
